TPU v7x, 128 devices: a whole 4x4x4 slice. The times are simulated.
128 devices in a mesh: tok: 4 (over y), seq: 16 (over z, x), kv: 2 (over core).
Axes of the slice: x: 4, y: 4, z: 4, core: 2. Of those that a mesh axis runs over, the one named last changes fastest.
Arguments:
- token_ids: int32 [64, 4], replicated, may hold values from 0 to 32767
- request_order: int32 [64], replicated, may hold values from 0 to 63, each once
- cache_lengths: int32 [64], replicated, may hold values from 1 to 16384, 524288 in all
- embed_table: bfloat16 [32768, 2048], P(('tok', 'kv'), 'seq'), may hold values from -3 to 3
- attn_gain: bfloat16 [2048], replicated, may hold values from 0.099609375 to 1.8984375
- proj_query: bfloat16 [2048, 2048], P(None, ('tok', 'kv')), may hold values from -0.125 to 0.125
- proj_kv: bfloat16 [2048, 8, 128], P(None, ('tok', 'kv')), may hold values from -0.125 to 0.125
- kv_cache: bfloat16 [64, 16384, 8, 128], P(None, 'seq', ('tok', 'kv')), may hold values from -125 to 125, as said below
- proj_out: bfloat16 [2048, 2048], P(('tok', 'kv'), 'seq'), may hold values from -0.25 to 0.25
- mlp_gain: bfloat16 [2048], replicated, may hold values from 0.099609375 to 1.8984375
- proj_gate: bfloat16 [2048, 8192], P(None, 'seq'), may hold values from -0.125 to 0.125
- proj_up: bfloat16 [2048, 8192], P(None, 'seq'), may hold values from -0.125 to 0.125
- proj_down: bfloat16 [8192, 2048], P('seq'), may hold values from -0.0625 to 0.0625
Outputs:
- hidden_out: bfloat16 [64, 4, 2048], P(('tok', 'kv'), None, 'seq')
Inputs may be any that keep to these rules, and one draw needn't show every extreme that they name: `request_order`: every request stands in exactly one slot. `cache_lengths`: the lengths sum to 524288 and the largest equals 16384. `kv_cache`: cached keys are already rotated to their positions.
All inputs are finite; a program needn't handle non-finite values.
Results may differ from a plain program's by a relative error of at most 0.018.
The roundings to bfloat16 on the way count: a program that leaves them out, or rounds other values in their place, can miss the bound.
Values may be sent and summed in bfloat16 or wider, within the bound.
A program may use at most 128 MiB of HBM per device.

v0:
```python
import jax
import jax.numpy as jnp
from jax import lax
from jax.sharding import PartitionSpec as P

EPSILON = 1e-05
ROPE_BASE = 1000000.0
FLOOR_SCORE = -1e30


def combined_all(value, axis, join):
    pieces = jax.tree.map(lambda part: lax.all_gather(part, axis), value)
    head = jax.tree.map(lambda part: part[0], pieces)
    tail = jax.tree.map(lambda part: part[1:], pieces)
    so_far, _ = lax.scan(lambda so_far, share: (join(so_far, share), None), head, tail)
    return so_far


def rotate(vector, position):
    half_dim = vector.shape[-1] // 2
    frequency = ROPE_BASE ** (-(jnp.arange(half_dim, dtype=jnp.float32) * 2.0 / vector.shape[-1]))
    angles = position[..., None] * frequency
    cosine = jnp.cos(angles)
    sine_part = jnp.sin(angles)
    front_half = vector[..., :half_dim]
    back_half = vector[..., half_dim:]
    return jnp.concatenate(
        [front_half * cosine - back_half * sine_part, back_half * cosine + front_half * sine_part],
        axis=-1,
    )


def combine(earlier, later):
    peak_a, mass_a, accum_a = earlier
    peak_b, mass_b, accum_b = later
    highest = jnp.maximum(peak_a, peak_b)
    factor_a = jnp.exp(peak_a - highest)
    factor_b = jnp.exp(peak_b - highest)
    return (
        highest,
        mass_a * factor_a + mass_b * factor_b,
        accum_a * factor_a[..., None] + accum_b * factor_b[..., None],
    )


def per_device(
    token_ids,
    request_order,
    cache_lengths,
    embed_table,
    attn_gain,
    proj_query,
    proj_kv,
    kv_cache,
    proj_out,
    mlp_gain,
    proj_gate,
    proj_up,
    proj_down,
):
    n_req, n_steps = token_ids.shape
    width = proj_query.shape[0]
    head_dim = kv_cache.shape[-1] // 2
    group_heads = proj_query.shape[1] // head_dim
    ctx_dev = kv_cache.shape[1]
    columns = embed_table.shape[1]
    vocab_rows = embed_table.shape[0]
    scale = head_dim ** (-0.5)
    owners = lax.axis_size("tok") * lax.axis_size("kv")
    owner_index = lax.axis_index("tok") * lax.axis_size("kv") + lax.axis_index("kv")
    seq_rank = lax.axis_index("seq")
    offset = token_ids.reshape(-1) - owner_index * vocab_rows
    inside = (offset >= 0) & (offset < vocab_rows)
    picked = jnp.take(embed_table, jnp.clip(offset, 0, vocab_rows - 1), axis=0)
    partial_x = jnp.where(inside[:, None], picked.astype(jnp.float32), 0.0)
    local_x = lax.psum(partial_x.astype(jnp.bfloat16), ("tok", "kv"))
    kv_flat = proj_kv.reshape(width, -1)
    full_x = lax.all_gather(local_x, "seq", axis=1, tiled=True)
    widened = full_x.astype(jnp.float32)
    square_mean = jnp.mean(widened * widened, axis=1)
    scaled = (widened * attn_gain.astype(jnp.float32)).astype(jnp.bfloat16)
    q_raw = jnp.dot(scaled, proj_query, preferred_element_type=jnp.float32)
    kv_raw = jnp.dot(scaled, kv_flat, preferred_element_type=jnp.float32)
    inv_norm = lax.rsqrt(square_mean + EPSILON)[:, None]
    q_scaled = (q_raw * inv_norm).reshape(n_req, n_steps, group_heads, head_dim)
    kv_scaled = (kv_raw * inv_norm).reshape(n_req, n_steps, 2 * head_dim)
    position = (cache_lengths[:, None] + jnp.arange(n_steps, dtype=jnp.int32)[None, :]).astype(
        jnp.float32
    )
    query = rotate(q_scaled, position[:, :, None]).astype(jnp.bfloat16)
    new_keys = rotate(kv_scaled[..., :head_dim], position).astype(jnp.bfloat16)
    new_values = kv_scaled[..., head_dim:].astype(jnp.bfloat16)
    cache_rows = kv_cache[:, :, 0, :]
    key_part = cache_rows[..., :head_dim]
    value_part = cache_rows[..., head_dim:]
    scores = (
        jnp.einsum("rjgd,rpd->rjgp", query, key_part, preferred_element_type=jnp.float32) * scale
    )
    places = seq_rank * ctx_dev + jnp.arange(ctx_dev, dtype=jnp.int32)
    is_live = (places[None, :] < cache_lengths[:, None])[:, None, None, :]
    masked = jnp.where(is_live, scores, FLOOR_SCORE)
    block_peak = jnp.max(masked, axis=-1)
    block_weight = jnp.where(is_live, jnp.exp(masked - block_peak[..., None]), 0.0).astype(
        jnp.bfloat16
    )
    block_mass = jnp.sum(block_weight.astype(jnp.float32), axis=-1)
    block_accum = jnp.einsum(
        "rjgp,rpd->rjgd", block_weight, value_part, preferred_element_type=jnp.float32
    )
    peak_all, mass_all, accum_all = combined_all(
        (block_peak, block_mass, block_accum), "seq", combine
    )
    fresh_scores = (
        jnp.einsum("rjgd,rkd->rjgk", query, new_keys, preferred_element_type=jnp.float32) * scale
    )
    causal = (jnp.arange(n_steps)[:, None] >= jnp.arange(n_steps)[None, :])[None, :, None, :]
    fresh_masked = jnp.where(causal, fresh_scores, FLOOR_SCORE)
    fresh_peak = jnp.max(fresh_masked, axis=-1)
    fresh_weight = jnp.where(causal, jnp.exp(fresh_masked - fresh_peak[..., None]), 0.0).astype(
        jnp.bfloat16
    )
    fresh_mass = jnp.sum(fresh_weight.astype(jnp.float32), axis=-1)
    fresh_accum = jnp.einsum(
        "rjgk,rkd->rjgd", fresh_weight, new_values, preferred_element_type=jnp.float32
    )
    highest = jnp.maximum(peak_all, fresh_peak)
    cache_factor = jnp.exp(peak_all - highest)
    fresh_factor = jnp.exp(fresh_peak - highest)
    numer = accum_all * cache_factor[..., None] + fresh_accum * fresh_factor[..., None]
    denom = mass_all * cache_factor + fresh_mass * fresh_factor
    attended = (
        (numer / denom[..., None])
        .astype(jnp.bfloat16)
        .reshape(n_req, n_steps, group_heads * head_dim)
    )
    slot_rows = attended[request_order].reshape(n_req * n_steps, group_heads * head_dim)
    per_owner = n_req // owners
    attn_part = lax.psum_scatter(
        jnp.dot(slot_rows, proj_out, preferred_element_type=jnp.float32),
        ("tok", "kv"),
        scatter_dimension=0,
        tiled=True,
    )
    my_requests = lax.dynamic_slice_in_dim(request_order, owner_index * per_owner, per_owner)
    own_x = local_x.reshape(n_req, n_steps, columns)[my_requests].reshape(
        per_owner * n_steps, columns
    )
    mid = (own_x.astype(jnp.float32) + attn_part).astype(jnp.bfloat16)
    piece_wide = lax.all_gather(mid, "seq", axis=1, tiled=True).astype(jnp.float32)
    gain_part = mlp_gain.astype(jnp.float32)
    piece_scaled = (piece_wide * gain_part).astype(jnp.bfloat16)
    gate_acc = jnp.dot(piece_scaled, proj_gate, preferred_element_type=jnp.float32)
    up_acc = jnp.dot(piece_scaled, proj_up, preferred_element_type=jnp.float32)
    square_total = jnp.sum(piece_wide * piece_wide, axis=1)
    inv_mlp = lax.rsqrt(square_total / width + EPSILON)[:, None]
    hidden = (jax.nn.silu(gate_acc * inv_mlp) * (up_acc * inv_mlp)).astype(jnp.bfloat16)
    down_terms = jnp.dot(hidden, proj_down, preferred_element_type=jnp.float32)
    mlp_part = lax.psum_scatter(down_terms, "seq", scatter_dimension=1, tiled=True)
    result = (mid.astype(jnp.float32) + mlp_part).astype(jnp.bfloat16)
    return result.reshape(per_owner, n_steps, columns)


def solution(mesh):
    placed = (
        P(),
        P(),
        P(),
        P(("tok", "kv"), "seq"),
        P(),
        P(None, ("tok", "kv")),
        P(None, ("tok", "kv"), None),
        P(None, "seq", ("tok", "kv"), None),
        P(("tok", "kv"), "seq"),
        P(),
        P(None, "seq"),
        P(None, "seq"),
        P("seq", None),
    )
    return jax.shard_map(
        per_device,
        mesh=mesh,
        in_specs=placed,
        out_specs=P(("tok", "kv"), None, "seq"),
        check_vma=False,
    )
```

profile of v0, /device:TPU:0, one launch (start us, length us, event | category | flops | bytes accessed | tf_op | source)
XLA Modules:
  0.0 429.6 jit_solution(7146980658867892863)
XLA Ops:
  6.5 0.8 compare_and_fusion.1
  8.7 2.1 gather_fusion
  11.6 61.3 %all-reduce.2.cloned.1.call-done = bf16[256,128]{1,0:T(8,128)(2,1)} async-done(((bf16[256,128]{1,0:T(8,128)(2,1)}), bf16[256,128]{1,0:T(8,128)(2,1)}) %all-reduce.2.cloned.1.call-update) | async-done | bytes 65552 | tf_op jit(solution)/shard_map/psum | solution.py:76
  73.6 22.1 %copy.87 = bf16[64,1024,1,128]{1,3,0,2:T(8,128)(2,1)} copy(bf16[64,1024,1,128]{3,1,2,0:T(8,128)(2,1)} %param.22) | data formatting | bytes 33554432 | tf_op args[7]
  96.5 21.2 %all-gather.6.cloned.1.call-done = bf16[256,2048]{1,0:T(8,128)(2,1)} async-done(((bf16[256,128]{1,0:T(8,128)(2,1)}), bf16[256,2048]{1,0:T(8,128)(2,1)}) %all-gather.6.cloned.1.call-update) | async-done | bytes 1048592 | tf_op jit(solution)/shard_map/all_gather | solution.py:78
  117.7 1.5 fusion.7
  119.2 2.0 convolution_multiply_fusion.1
  121.4 1.8 convolution_multiply_fusion.2
  123.5 1.0 multiply_cosine_fusion
  125.2 6.2 %fusion.5 = (f32[64,4,4]{2,1,0:T(4,128)S(1)}, f32[64,4,4,1024]{3,2,1,0:T(4,128)S(1)}) fusion(pred[64,1024]{1,0:T(8,128)(4,1)} %broadcast_compare_fusion, bf16[64,1024,128]{1,2,0:T(8,128)(2,1)} %bitcast.67, bf16[64,4,4,32]{3,2,1,0:T(4,128)(2,1)S(1)} %get-tuple-element.101, bf16[64,4,4,32]{3,2,1,0:T(4,128)(2,1)S(1)} %get-tuple-element.100), kind=kOutput, calls=%fused_computation.18 | convolution fusion | flops 137624576 | bytes 12783616 | tf_op jit(solution)/shard_map/rjgd,rpd->rjgp/dot_general | solution.py:97
  131.4 3.7 convert_reduce_fusion
  135.1 6.8 %fusion.3 = f32[64,4,4,64]{3,2,1,0:T(4,128)} fusion(bf16[64,4,4,1024]{3,2,1,0:T(4,128)(2,1)S(1)} %get-tuple-element.99, bf16[64,1024,128]{1,2,0:T(8,128)(2,1)} %bitcast.68), kind=kOutput, calls=%fused_computation.12 | convolution fusion | flops 134217728 | bytes 10747904 | tf_op jit(solution)/shard_map/rjgp,rpd->rjgd/dot_general | solution.py:107
  142.7 30.8 %all-gather.1 = f32[1024,4,4]{2,1,0:T(4,128)S(1)} all-gather(f32[64,4,4]{2,1,0:T(4,128)S(1)} %get-tuple-element.98), channel_id=3, replica_groups=mesh['tok'=4,'seq'=16,'kv'=2] {'seq'}, dimensions={0}, use_global_device_ids=true | all-gather | bytes 69632 | tf_op jit(solution)/shard_map/all_gather | solution.py:12
  173.5 1.4 slice.76
  174.9 32.0 %all-gather = f32[1024,4,4]{2,1,0:T(4,128)S(1)} all-gather(f32[64,4,4]{2,1,0:T(4,128)S(1)} %get-tuple-element.110), channel_id=2, replica_groups=mesh['tok'=4,'seq'=16,'kv'=2] {'seq'}, dimensions={0}, use_global_device_ids=true | all-gather | bytes 69632 | tf_op jit(solution)/shard_map/all_gather | solution.py:12
  206.9 1.4 slice.75
  209.1 3.3 fusion.36
  213.6 1.0 copy.102
  214.6 2.7 copy.93
  217.4 2.2 copy.92
  219.6 5.8 %all-gather.8.cloned.1.call-done = f32[1024,4,4,64]{3,2,1,0:T(4,128)} async-done(((f32[64,4,4,64]{3,2,1,0:T(4,128)}), f32[1024,4,4,64]{3,2,1,0:T(4,128)}) %all-gather.8.cloned.1.call-update) | async-done | bytes 4194320 | tf_op jit(solution)/shard_map/all_gather | solution.py:12
  225.3 7.7 %slice.77 = f32[960,4,4,64]{3,2,1,0:T(4,128)} slice(f32[1024,4,4,64]{3,2,1,0:T(4,128)} %all-gather.8.cloned.1.call-done), slice={[64:1024], [0:4], [0:4], [0:64]} | slice | bytes 7864320 | tf_op jit(solution)/shard_map/slice | solution.py:14
  233.1 53.9 %while.14 = (s32[]{:T(128)}, f32[64,4,4]{0,2,1:T(4,128)S(1)}, f32[64,4,4]{0,2,1:T(4,128)S(1)}, f32[64,4,4,64]{3,2,1,0:T(4,128)S(1)}, f32[15,64,4,4]{1,3,2,0:T(4,...) while((s32[]{:T(128)}, f32[64,4,4]{0,2,1:T(4,128)S(1)}, ...), condition=%wide.region_5.6_spmd, body=%wide.region_4.5_spmd.sunk | while | flops 202754 | bytes 843877 | solution.py:15
  234.1 2.6 fusion.54
  237.7 2.6 fusion.54
  241.3 2.6 fusion.54
  244.9 2.6 fusion.54
  248.5 2.6 fusion.54
  252.1 2.6 fusion.54
  255.7 2.6 fusion.54
  259.2 2.6 fusion.54
  262.8 2.6 fusion.54
  266.4 2.6 fusion.54
  270.0 2.6 fusion.54
  273.6 2.6 fusion.54
  277.2 2.6 fusion.54
  280.8 2.6 fusion.54
  284.4 2.6 fusion.54
  288.7 2.0 fusion.10
  290.9 0.8 gather_fusion.2
  291.8 0.8 fusion.41
  292.8 1.4 gather_fusion.1
  294.2 28.3 %reduce-scatter.3.cloned.1.call-done = f32[32,128]{1,0:T(8,128)} async-done(((f32[256,128]{1,0:T(8,128)}), f32[32,128]{1,0:T(8,128)}) %reduce-scatter.3.cloned.1.call-update) | async-done | bytes 16400 | tf_op jit(solution)/shard_map/reduce_scatter | solution.py:138
  323.3 23.9 %all_gather.31 = bf16[32,2048]{1,0:T(8,128)(2,1)S(1)} all-gather(bf16[32,128]{1,0:T(8,128)(2,1)S(1)} %fusion.32), channel_id=1, replica_groups=mesh['tok'=4,'seq'=16,'kv'=2] {'seq'}, dimensions={1}, use_global_device_ids=true | all-gather | bytes 139264 | tf_op jit(solution)/shard_map/all_gather | solution.py:149
  347.3 2.0 convolution_multiply_fusion.4
  349.4 3.2 fusion.13
  352.6 69.2 %reduce-scatter.5.cloned.1.call-done = f32[32,128]{1,0:T(8,128)} async-done(((f32[32,2048]{1,0:T(8,128)}), f32[32,128]{1,0:T(8,128)}) %reduce-scatter.5.cloned.1.call-update) | async-done | bytes 16400 | tf_op jit(solution)/shard_map/reduce_scatter | solution.py:158
  421.8 1.3 add_convert_fusion.2
  (126 shorter events, 25.5 us)
Async XLA Ops:
  6.5 342.8 %copy-start = (bf16[512,2048]{1,0:T(8,128)(2,1)S(1)}, bf16[512,2048]{1,0:T(8,128)(2,1)}, u32[]{:S(2)}) copy-start(bf16[512,2048]{1,0:T(8,128)(2,1)} %param.27) | copy-start | bytes 6291460
  6.5 66.3 %all-reduce.2.cloned.1.call-start = ((), (), s32[]{:S(2)}) async-start(), calls=%async_computation.2 | async-start | bytes 131072 | tf_op jit(solution)/shard_map/psum | solution.py:76
  11.5 106.1 %all-gather.6.cloned.1.call-start = ((), (), s32[]{:S(2)}) async-start(), calls=%async_computation.3 | async-start | bytes 1114112 | tf_op jit(solution)/shard_map/all_gather | solution.py:78
  72.9 152.4 %all-gather.8.cloned.1.call-start = ((), (), s32[]{:S(2)}) async-start(), calls=%async_computation.6 | async-start | bytes 8912896 | tf_op jit(solution)/shard_map/all_gather | solution.py:12
  73.6 22.1 %copy-start.7 = (s32[64]{0:T(128)S(1)}, s32[64]{0:T(128)}, u32[]{:S(2)}) copy-start(s32[64]{0:T(128)} %param.17) | copy-start | bytes 772
  125.2 6.2 %copy-start.1 = (pred[64,1024]{1,0:T(8,128)(4,1)S(1)}, pred[64,1024]{1,0:T(8,128)(4,1)}, u32[]{:S(2)}) copy-start(pred[64,1024]{1,0:T(8,128)(4,1)} %broadcast_compare_fusion) | copy-start | bytes 196612
  135.1 6.9 %copy-start.9 = (s32[64]{0:T(128)S(1)}, s32[64]{0:T(128)}, u32[]{:S(2)}) copy-start(s32[64]{0:T(128)} %param.16) | copy-start | bytes 772
  142.0 180.5 %reduce-scatter.3.cloned.1.call-start = ((), (), s32[]{:S(2)}) async-start(), calls=%async_computation.4 | async-start | bytes 147456 | tf_op jit(solution)/shard_map/reduce_scatter | solution.py:138
  142.1 70.6 %copy-start.8 = (pred[4,4]{1,0:T(4,128)(4,1)}, pred[4,4]{1,0:T(4,128)(4,1)S(1)}, u32[]{:S(2)}) copy-start(pred[4,4]{1,0:T(4,128)(4,1)S(1)} %iota_compare_fusion) | copy-start | bytes 52
  174.9 33.4 %copy-start.3 = (bf16[64,4,32]{0,2,1:T(8,128)(2,1)S(1)}, bf16[64,4,32]{0,2,1:T(8,128)(2,1)}, u32[]{:S(2)}) copy-start(bf16[64,4,32]{0,2,1:T(8,128)(2,1)} %get-tuple-element.108) | copy-start | bytes 49156
  174.9 33.4 %copy-start.4 = (bf16[64,4,32]{0,2,1:T(8,128)(2,1)S(1)}, bf16[64,4,32]{0,2,1:T(8,128)(2,1)}, u32[]{:S(2)}) copy-start(bf16[64,4,32]{0,2,1:T(8,128)(2,1)} %get-tuple-element.109) | copy-start | bytes 49156
  225.3 7.7 %slice-start = ((f32[1024,4,4,64]{3,2,1,0:T(4,128)}), f32[64,4,4,64]{3,2,1,0:T(4,128)S(1)}, s32[]{:S(2)}) async-start(f32[1024,4,4,64]{3,2,1,0:T(4,128)} %all-gather.8.cloned.1.call-done), calls=%async_computation.7 | async-start | bytes 1048576 | tf_op jit(solution)/shard_map/slice | solution.py:13
  233.1 55.7 %copy-start.2 = (bf16[64,4,4,4]{3,2,1,0:T(4,128)(2,1)S(1)}, bf16[64,4,4,4]{3,2,1,0:T(4,128)(2,1)}, u32[]{:S(2)}) copy-start(bf16[64,4,4,4]{3,2,1,0:T(4,128)(2,1)} %copy.102) | copy-start | bytes 24580
  288.7 3.1 copy-start.5
  288.7 4.0 copy-start.6
  288.7 4.0 copy-start.10
  292.6 129.1 %reduce-scatter.5.cloned.1.call-start = ((), (), s32[]{:S(2)}) async-start(), calls=%async_computation.5 | async-start | bytes 278528 | tf_op jit(solution)/shard_map/reduce_scatter | solution.py:158
Sparse Core Ops, SparseCore 0:
  11.7 61.1 all-reduce.1
  75.2 42.4 all-gather.5
  142.1 83.1 all-gather.7
  292.8 29.7 reduce-scatter.2
  352.7 68.9 reduce-scatter.4
where the time goes:
time: 432 us; the launch traced here: 430 us
  waiting for transfers between devices  186 us (43%)
  blocking collectives  86.6 us (20%)
  other arithmetic  63.8 us (15%)
  local copies, waits for them, and re-layouts  51.2 us (12%)
  matrix products  28.1 us (7%)
  between operations  13.4 us (3%)
    reduce_scatter x1, waiting for transfers between devices, per_device(): lax.psum_scatter(down_terms, 'seq', scatter_dimension=1, tiled=True)  69.2 us
    all_gather x2, blocking collectives, combined_all(): pieces = jax.tree.map(lambda part: lax.all_gather(part, axis), value)  62.8 us
    psum x1, waiting for transfers between devices, per_device(): local_x = lax.psum(partial_x.astype(jnp.bfloat16), ('tok', 'kv'))  61.3 us
    add x15, other arithmetic, combine(): accum_a * factor_a[..., None] + accum_b * factor_b[..., None]  38.7 us
    reduce_scatter x1, waiting for transfers between devices, per_device(): lax.psum_scatter(jnp.dot(slot_rows, proj_out, preferred_element_type=jnp....  28.3 us
    all_gather x1, blocking collectives, per_device(): lax.all_gather(mid, 'seq', axis=1, tiled=True).astype(jnp.float32)  23.9 us
    unnamed x25, local copies, waits for them, and re-layouts  22.3 us
    all_gather x1, waiting for transfers between devices, per_device(): full_x = lax.all_gather(local_x, 'seq', axis=1, tiled=True)  21.2 us
  transfers between devices with their start and end apart: 5, of which 5 were waited for; matrix products, arithmetic and copies ran while one was open for 9% of the time, Pallas kernels for 0%

commit v1 on v0

--- a/solution.py
+++ b/solution.py
@@ -1,3 +1,4 @@
+import functools
 import jax
 import jax.numpy as jnp
 from jax import lax
@@ -6,6 +7,13 @@
 EPSILON = 1e-05
 ROPE_BASE = 1000000.0
 FLOOR_SCORE = -1e30
+
+
+def strips_all_lay(x_part, lane_axis):
+    return lax.all_gather(x_part, lane_axis).sum(axis=0)
+
+
+divide_map = functools.partial(strips_all_lay, lane_axis=("tok", "kv"))
 
 
 def combined_all(value, axis, join):
@@ -73,7 +81,7 @@
     inside = (offset >= 0) & (offset < vocab_rows)
     picked = jnp.take(embed_table, jnp.clip(offset, 0, vocab_rows - 1), axis=0)
     partial_x = jnp.where(inside[:, None], picked.astype(jnp.float32), 0.0)
-    local_x = lax.psum(partial_x.astype(jnp.bfloat16), ("tok", "kv"))
+    local_x = divide_map(partial_x.astype(jnp.bfloat16))
     kv_flat = proj_kv.reshape(width, -1)
     full_x = lax.all_gather(local_x, "seq", axis=1, tiled=True)
     widened = full_x.astype(jnp.float32)

time: 432 us -> 385 us (0.89)
  waiting for transfers between devices: 186 us -> 125 us
  blocking collectives: 86.6 us -> 100 us
    psum x1 -> x0, waiting for transfers between devices: 61.3 us -> none  [per_device(): local_x = lax.psum(partial_x.astype(jnp.bfloat16), ('tok', 'kv'))]
    all_gather x0 -> x1, blocking collectives: none -> 13.7 us  [strips_all_lay(): return lax.all_gather(x_part, lane_axis).sum(axis=0)]
  transfers between devices with their start and end apart: 5 -> 4, of which waited for: 5 -> 4; matrix products, arithmetic and copies ran while one was open for 9% -> 10% of each run, Pallas kernels for 0% -> 0%
where the time goes in v1:
time: 385 us; the launch traced here: 382 us
  waiting for transfers between devices  125 us (32%)
  blocking collectives  100 us (26%)
  other arithmetic  64 us (17%)
  local copies, waits for them, and re-layouts  51.5 us (13%)
  matrix products  28.1 us (7%)
  between operations  13.4 us (3%)
    reduce_scatter x1, waiting for transfers between devices, per_device(): lax.psum_scatter(down_terms, 'seq', scatter_dimension=1, tiled=True)  69 us
    all_gather x2, blocking collectives, combined_all(): pieces = jax.tree.map(lambda part: lax.all_gather(part, axis), value)  62.8 us
    add x15, other arithmetic, combine(): accum_a * factor_a[..., None] + accum_b * factor_b[..., None]  38.7 us
    reduce_scatter x1, waiting for transfers between devices, per_device(): lax.psum_scatter(jnp.dot(slot_rows, proj_out, preferred_element_type=jnp....  28.3 us
    all_gather x1, blocking collectives, per_device(): lax.all_gather(mid, 'seq', axis=1, tiled=True).astype(jnp.float32)  23.8 us
    unnamed x25, local copies, waits for them, and re-layouts  22.6 us
    all_gather x1, waiting for transfers between devices, per_device(): full_x = lax.all_gather(local_x, 'seq', axis=1, tiled=True)  21.5 us
    all_gather x1, blocking collectives, strips_all_lay(): return lax.all_gather(x_part, lane_axis).sum(axis=0)  13.7 us
  transfers between devices with their start and end apart: 4, of which 4 were waited for; matrix products, arithmetic and copies ran while one was open for 10% of the time, Pallas kernels for 0%

profile of v1, /device:TPU:0, one launch (start us, length us, event | category | flops | bytes accessed | tf_op | source)
XLA Modules:
  0.0 382.4 jit_solution(11328825159960691946)
XLA Ops:
  6.5 0.8 compare_and_fusion.1
  8.7 2.1 gather_fusion
  10.9 13.7 %all_gather.28 = bf16[8,256,128]{2,1,0:T(8,128)(2,1)S(1)} all-gather(bf16[1,256,128]{2,1,0:T(8,128)(2,1)S(1)} %select_convert_fusion.1), channel_id=1, replica_groups=mesh['tok'=4,'seq'=16,'kv'=2] {'tok','kv'}, dimensions={0}, use_global_device_ids=true | all-gather | bytes 589824 | tf_op jit(solution)/shard_map/all_gather | solution.py:13
  26.1 22.4 %copy.103 = bf16[64,1024,1,128]{1,3,0,2:T(8,128)(2,1)} copy(bf16[64,1024,1,128]{3,1,2,0:T(8,128)(2,1)} %param.22) | data formatting | bytes 33554432 | tf_op args[7]
  49.2 21.5 %all-gather.6.cloned.1.call-done = bf16[256,2048]{1,0:T(8,128)(2,1)} async-done(((bf16[256,128]{1,0:T(8,128)(2,1)}), bf16[256,2048]{1,0:T(8,128)(2,1)}) %all-gather.6.cloned.1.call-update) | async-done | bytes 1048592 | tf_op jit(solution)/shard_map/all_gather | solution.py:86
  70.7 1.5 fusion.7
  72.2 2.0 convolution_multiply_fusion.1
  74.4 1.8 convolution_multiply_fusion.2
  76.5 1.0 multiply_cosine_fusion
  78.2 6.1 %fusion.5 = (f32[64,4,4]{2,1,0:T(4,128)S(1)}, f32[64,4,4,1024]{3,2,1,0:T(4,128)S(1)}) fusion(pred[64,1024]{1,0:T(8,128)(4,1)} %broadcast_compare_fusion, bf16[64,1024,128]{1,2,0:T(8,128)(2,1)} %bitcast.71, bf16[64,4,4,32]{3,2,1,0:T(4,128)(2,1)S(1)} %get-tuple-element.108, bf16[64,4,4,32]{3,2,1,0:T(4,128)(2,1)S(1)} %get-tuple-element.107), kind=kOutput, calls=%fused_computation.18 | convolution fusion | flops 137624576 | bytes 12783616 | tf_op jit(solution)/shard_map/rjgd,rpd->rjgp/dot_general | solution.py:105
  84.4 3.7 convert_reduce_fusion
  88.1 6.8 %fusion.3 = f32[64,4,4,64]{3,2,1,0:T(4,128)} fusion(bf16[64,4,4,1024]{3,2,1,0:T(4,128)(2,1)S(1)} %get-tuple-element.106, bf16[64,1024,128]{1,2,0:T(8,128)(2,1)} %bitcast.72), kind=kOutput, calls=%fused_computation.12 | convolution fusion | flops 134217728 | bytes 10747904 | tf_op jit(solution)/shard_map/rjgp,rpd->rjgd/dot_general | solution.py:115
  95.7 30.8 %all-gather.1 = f32[1024,4,4]{2,1,0:T(4,128)S(1)} all-gather(f32[64,4,4]{2,1,0:T(4,128)S(1)} %get-tuple-element.105), channel_id=3, replica_groups=mesh['tok'=4,'seq'=16,'kv'=2] {'seq'}, dimensions={0}, use_global_device_ids=true | all-gather | bytes 69632 | tf_op jit(solution)/shard_map/all_gather | solution.py:20
  126.5 1.4 slice.76
  127.9 32.0 %all-gather = f32[1024,4,4]{2,1,0:T(4,128)S(1)} all-gather(f32[64,4,4]{2,1,0:T(4,128)S(1)} %get-tuple-element.117), channel_id=2, replica_groups=mesh['tok'=4,'seq'=16,'kv'=2] {'seq'}, dimensions={0}, use_global_device_ids=true | all-gather | bytes 69632 | tf_op jit(solution)/shard_map/all_gather | solution.py:20
  159.9 1.5 slice.75
  162.1 3.3 fusion.36
  166.7 1.0 copy.118
  167.7 2.7 copy.109
  170.5 2.2 copy.108
  172.6 5.7 %all-gather.8.cloned.1.call-done = f32[1024,4,4,64]{3,2,1,0:T(4,128)} async-done(((f32[64,4,4,64]{3,2,1,0:T(4,128)}), f32[1024,4,4,64]{3,2,1,0:T(4,128)}) %all-gather.8.cloned.1.call-update) | async-done | bytes 4194320 | tf_op jit(solution)/shard_map/all_gather | solution.py:20
  178.3 7.7 %slice.77 = f32[960,4,4,64]{3,2,1,0:T(4,128)} slice(f32[1024,4,4,64]{3,2,1,0:T(4,128)} %all-gather.8.cloned.1.call-done), slice={[64:1024], [0:4], [0:4], [0:64]} | slice | bytes 7864320 | tf_op jit(solution)/shard_map/slice | solution.py:22
  186.1 53.9 %while.14 = (s32[]{:T(128)}, f32[64,4,4]{0,2,1:T(4,128)S(1)}, f32[64,4,4]{0,2,1:T(4,128)S(1)}, f32[64,4,4,64]{3,2,1,0:T(4,128)S(1)}, f32[15,64,4,4]{1,3,2,0:T(4,...) while((s32[]{:T(128)}, f32[64,4,4]{0,2,1:T(4,128)S(1)}, ...), condition=%wide.region_5.6_spmd, body=%wide.region_4.5_spmd.sunk | while | flops 202754 | bytes 843877 | solution.py:23
  187.1 2.6 fusion.54
  190.7 2.6 fusion.54
  194.3 2.6 fusion.54
  197.9 2.6 fusion.54
  201.5 2.6 fusion.54
  205.1 2.6 fusion.54
  208.7 2.6 fusion.54
  212.3 2.6 fusion.54
  215.9 2.6 fusion.54
  219.4 2.6 fusion.54
  223.0 2.6 fusion.54
  226.6 2.6 fusion.54
  230.2 2.6 fusion.54
  233.8 2.6 fusion.54
  237.4 2.6 fusion.54
  241.7 2.0 fusion.10
  243.9 0.8 gather_fusion.2
  244.8 0.8 fusion.41
  245.8 1.4 gather_fusion.1
  247.2 28.3 %reduce-scatter.3.cloned.1.call-done = f32[32,128]{1,0:T(8,128)} async-done(((f32[256,128]{1,0:T(8,128)}), f32[32,128]{1,0:T(8,128)}) %reduce-scatter.3.cloned.1.call-update) | async-done | bytes 16400 | tf_op jit(solution)/shard_map/reduce_scatter | solution.py:146
  276.3 23.8 %all_gather.36 = bf16[32,2048]{1,0:T(8,128)(2,1)S(1)} all-gather(bf16[32,128]{1,0:T(8,128)(2,1)S(1)} %fusion.32), channel_id=1, replica_groups=mesh['tok'=4,'seq'=16,'kv'=2] {'seq'}, dimensions={1}, use_global_device_ids=true | all-gather | bytes 139264 | tf_op jit(solution)/shard_map/all_gather | solution.py:157
  300.3 2.0 convolution_multiply_fusion.4
  302.4 3.2 fusion.13
  305.6 69.0 %reduce-scatter.5.cloned.1.call-done = f32[32,128]{1,0:T(8,128)} async-done(((f32[32,2048]{1,0:T(8,128)}), f32[32,128]{1,0:T(8,128)}) %reduce-scatter.5.cloned.1.call-update) | async-done | bytes 16400 | tf_op jit(solution)/shard_map/reduce_scatter | solution.py:166
  374.6 1.3 add_convert_fusion.2
  (125 shorter events, 25.6 us)
Async XLA Ops:
  6.5 295.8 %copy-start = (bf16[512,2048]{1,0:T(8,128)(2,1)S(1)}, bf16[512,2048]{1,0:T(8,128)(2,1)}, u32[]{:S(2)}) copy-start(bf16[512,2048]{1,0:T(8,128)(2,1)} %param.27) | copy-start | bytes 6291460
  6.5 64.1 %all-gather.6.cloned.1.call-start = ((), (), s32[]{:S(2)}) async-start(), calls=%async_computation.2 | async-start | bytes 1114112 | tf_op jit(solution)/shard_map/all_gather | solution.py:86
  25.3 153.0 %all-gather.8.cloned.1.call-start = ((), (), s32[]{:S(2)}) async-start(), calls=%async_computation.5 | async-start | bytes 8912896 | tf_op jit(solution)/shard_map/all_gather | solution.py:20
  26.1 22.4 %copy-start.7 = (s32[64]{0:T(128)S(1)}, s32[64]{0:T(128)}, u32[]{:S(2)}) copy-start(s32[64]{0:T(128)} %param.17) | copy-start | bytes 772
  78.2 6.2 %copy-start.1 = (pred[64,1024]{1,0:T(8,128)(4,1)S(1)}, pred[64,1024]{1,0:T(8,128)(4,1)}, u32[]{:S(2)}) copy-start(pred[64,1024]{1,0:T(8,128)(4,1)} %broadcast_compare_fusion) | copy-start | bytes 196612
  88.1 6.9 %copy-start.9 = (s32[64]{0:T(128)S(1)}, s32[64]{0:T(128)}, u32[]{:S(2)}) copy-start(s32[64]{0:T(128)} %param.16) | copy-start | bytes 772
  95.0 180.6 %reduce-scatter.3.cloned.1.call-start = ((), (), s32[]{:S(2)}) async-start(), calls=%async_computation.3 | async-start | bytes 147456 | tf_op jit(solution)/shard_map/reduce_scatter | solution.py:146
  95.1 70.7 %copy-start.8 = (pred[4,4]{1,0:T(4,128)(4,1)}, pred[4,4]{1,0:T(4,128)(4,1)S(1)}, u32[]{:S(2)}) copy-start(pred[4,4]{1,0:T(4,128)(4,1)S(1)} %iota_compare_fusion) | copy-start | bytes 52
  127.9 33.5 %copy-start.3 = (bf16[64,4,32]{0,2,1:T(8,128)(2,1)S(1)}, bf16[64,4,32]{0,2,1:T(8,128)(2,1)}, u32[]{:S(2)}) copy-start(bf16[64,4,32]{0,2,1:T(8,128)(2,1)} %get-tuple-element.115) | copy-start | bytes 49156
  127.9 33.5 %copy-start.4 = (bf16[64,4,32]{0,2,1:T(8,128)(2,1)S(1)}, bf16[64,4,32]{0,2,1:T(8,128)(2,1)}, u32[]{:S(2)}) copy-start(bf16[64,4,32]{0,2,1:T(8,128)(2,1)} %get-tuple-element.116) | copy-start | bytes 49156
  178.3 7.7 %slice-start = ((f32[1024,4,4,64]{3,2,1,0:T(4,128)}), f32[64,4,4,64]{3,2,1,0:T(4,128)S(1)}, s32[]{:S(2)}) async-start(f32[1024,4,4,64]{3,2,1,0:T(4,128)} %all-gather.8.cloned.1.call-done), calls=%async_computation.6 | async-start | bytes 1048576 | tf_op jit(solution)/shard_map/slice | solution.py:21
  186.1 55.7 %copy-start.2 = (bf16[64,4,4,4]{3,2,1,0:T(4,128)(2,1)S(1)}, bf16[64,4,4,4]{3,2,1,0:T(4,128)(2,1)}, u32[]{:S(2)}) copy-start(bf16[64,4,4,4]{3,2,1,0:T(4,128)(2,1)} %copy.118) | copy-start | bytes 24580
  241.7 3.1 copy-start.5
  241.7 4.0 %copy-start.6 = (bf16[2048]{0:T(1024)(128)(2,1)S(1)}, bf16[2048]{0:T(1024)(128)(2,1)}, u32[]{:S(2)}) copy-start(bf16[2048]{0:T(1024)(128)(2,1)} %param.24) | copy-start | bytes 12292
  241.7 4.0 %copy-start.10 = (s32[64]{0:T(128)S(1)}, s32[64]{0:T(128)}, u32[]{:S(2)}) copy-start(s32[64]{0:T(128)} %param.16) | copy-start | bytes 772
  245.7 128.9 %reduce-scatter.5.cloned.1.call-start = ((), (), s32[]{:S(2)}) async-start(), calls=%async_computation.4 | async-start | bytes 278528 | tf_op jit(solution)/shard_map/reduce_scatter | solution.py:166
Sparse Core Ops, SparseCore 0:
  25.4 45.2 all-gather.5
  95.1 83.1 all-gather.7
  245.8 29.7 reduce-scatter.2
  305.7 68.8 reduce-scatter.4
